TPU v7x, 32 devices: a whole 2x2x4 slice. The times are simulated.
32 devices in a mesh: stn: 4 (over y, x), chan: 4 (over z), beam: 2 (over core).
Axes of the slice: x: 2, y: 2, z: 4, core: 2. Of those that a mesh axis runs over, the one named last changes fastest.
Arguments:
- volts: bfloat16 [2, 128, 12, 9216], P(None, 'stn', 'chan', 'beam'), may hold values from -6 to 6
- taps: float32 [16, 256], replicated, may hold values from -1.5 to 1.5
- delays: int32 [32, 128], P(None, 'stn'), may hold values from 0 to 1023
- station_sub: int32 [128], P('stn'), may hold values from 0 to 3
- beam_sub: int32 [32], replicated, may hold values from 0 to 3
Outputs:
- beams: float32 [32, 2, 12, 48, 256], P(('stn', 'chan', 'beam'))
All inputs are finite; a program needn't handle non-finite values.
Results may differ from a plain program's by a relative error of at most 0.014.
Values may be sent and summed in bfloat16 or wider, within the bound.
A program may use at most 192 MiB of HBM per device.

v0:
```python
import math

import jax
import jax.numpy as jnp
from jax import lax
from jax.sharding import PartitionSpec as P

SUBARRAYS = 4


def shifted(block, axis, distance):
    devices = range(lax.axis_size(axis))
    route = [(i - distance, i) for i in devices if i - distance in devices]
    return lax.ppermute(block, axis, route)


def filter_frames(extended, taps, frame_count):
    tap_count, fine = taps.shape
    hop = 3 * fine // 4
    groups = frame_count // 4
    rows = groups + (tap_count + 2) // 3
    shape = extended.shape
    needed = 3 * hop + 3 * rows * fine
    padding = max(0, needed - shape[-1])
    padded = jnp.concatenate(
        [extended, jnp.zeros(shape[:-1] + (padding,), extended.dtype)], axis=-1
    )
    streams = []
    for phase in range(4):
        start = phase * hop
        piece = lax.slice_in_dim(padded, start, start + 3 * rows * fine, 1, len(shape) - 1)
        streams.append(piece.reshape(shape[:-1] + (rows, 3, fine)))
    stacked = jnp.stack(streams, axis=-2)
    axis = len(shape) - 1
    total = None
    for tap in range(tap_count):
        lead = tap // 3
        inner = tap % 3
        window = lax.slice_in_dim(stacked, lead, lead + groups, 1, axis)[..., inner, :, :].astype(
            jnp.float32
        )
        term = taps[tap] * window
        total = term if total is None else total + term
    return total.reshape(shape[:-1] + (frame_count, fine)).astype(jnp.bfloat16)


def dft_tables(fine):
    index = jnp.arange(fine, dtype=jnp.int32)
    product = index[:, None] * index[None, :] % fine
    angle = 2.0 * jnp.pi * product.astype(jnp.float32) / fine
    scale = 1.0 / math.sqrt(fine)
    return (
        (jnp.cos(angle) * scale).astype(jnp.bfloat16),
        (jnp.sin(angle) * scale).astype(jnp.bfloat16),
    )


def channelize(filtered, frame_start, hop):
    fine = filtered.shape[-1]
    cosine, sine = dft_tables(fine)
    spec_re = jnp.einsum(
        "...j,jk->...k", filtered[0], cosine, preferred_element_type=jnp.float32
    ) + jnp.einsum("...j,jk->...k", filtered[1], sine, preferred_element_type=jnp.float32)
    spec_im = jnp.einsum(
        "...j,jk->...k", filtered[1], cosine, preferred_element_type=jnp.float32
    ) - jnp.einsum("...j,jk->...k", filtered[0], sine, preferred_element_type=jnp.float32)
    frame_count = filtered.shape[-2]
    frame_index = frame_start + jnp.arange(frame_count, dtype=jnp.int32)
    fine_index = jnp.arange(fine, dtype=jnp.int32)
    turn = fine_index[None, :] * hop % fine * frame_index[:, None] % fine
    rot = 2.0 * jnp.pi * turn.astype(jnp.float32) / fine
    cos_rot = jnp.cos(rot)
    sin_rot = jnp.sin(rot)
    out_re = spec_re * cos_rot + spec_im * sin_rot
    out_im = spec_im * cos_rot - spec_re * sin_rot
    return jnp.stack([out_re, out_im]).astype(jnp.bfloat16)


def steering_band(
    delay_rows, beam_subs, station_subs, chan_start, chan_count, fine, width, amplitude
):
    fine_index = jnp.arange(width, dtype=jnp.int32)
    chan_index = chan_start + jnp.arange(chan_count, dtype=jnp.int32)
    freq_index = chan_index[:, None] * fine + fine_index[None, :]
    turn = delay_rows[:, :, None, None] * freq_index[None, None, :, :] % 65536
    phase = 2.0 * jnp.pi * turn.astype(jnp.float32) / 65536.0
    member = (beam_subs[:, None] == station_subs[None, :]).astype(jnp.float32)[:, :, None, None]
    weight_re = (amplitude * member * jnp.cos(phase)).astype(jnp.bfloat16)
    weight_im = (-amplitude * member * jnp.sin(phase)).astype(jnp.bfloat16)
    return (weight_re, weight_im)


def complex_form(weight_re, weight_im, pieces):
    form = "bsck,scfk->bcfk"
    part_re = jnp.einsum(
        form, weight_re, pieces[0], preferred_element_type=jnp.float32
    ) - jnp.einsum(form, weight_im, pieces[1], preferred_element_type=jnp.float32)
    part_im = jnp.einsum(
        form, weight_re, pieces[1], preferred_element_type=jnp.float32
    ) + jnp.einsum(form, weight_im, pieces[0], preferred_element_type=jnp.float32)
    return jnp.stack([part_re, part_im], axis=1)


def body(volts, taps, delays, station_sub, beam_sub):
    tap_count, fine = taps.shape
    hop = 3 * fine // 4
    frames_dev = volts.shape[3] // hop
    chan_count = volts.shape[2]
    extra = tap_count * fine - hop
    tail = shifted(volts[:, :, :, :extra], "beam", -1)
    extended = jnp.concatenate([volts, tail], axis=3)
    chan_start = lax.axis_index("chan") * chan_count
    frame_start = lax.axis_index("beam") * frames_dev
    filtered = filter_frames(extended, taps, frames_dev)
    spectra = channelize(filtered, frame_start, hop)
    group_width = delays.shape[1]
    stn_size = lax.axis_size("stn")
    stations = group_width * stn_size
    amplitude = 1.0 / math.sqrt(stations // SUBARRAYS)
    weight_re, weight_im = steering_band(
        delays, beam_sub, station_sub, chan_start, chan_count, fine, fine, amplitude
    )
    summed = lax.psum_scatter(
        complex_form(weight_re, weight_im, spectra).astype(jnp.bfloat16),
        "stn",
        scatter_dimension=0,
        tiled=True,
    ).astype(jnp.float32)
    result = lax.all_to_all(
        lax.all_to_all(
            summed.astype(jnp.bfloat16), "chan", split_axis=0, concat_axis=2, tiled=True
        ),
        "beam",
        split_axis=0,
        concat_axis=3,
        tiled=True,
    ).astype(summed.dtype)
    return result


def solution(mesh):
    placed = (P(None, "stn", "chan", "beam"), P(), P(None, "stn"), P("stn"), P())
    return jax.shard_map(
        body,
        mesh=mesh,
        in_specs=placed,
        out_specs=P(("stn", "chan", "beam"), None, None, None, None),
        check_vma=False,
    )
```

profile of v0, /device:TPU:0, one launch (start us, length us, event | category | flops | bytes accessed | tf_op | source)
XLA Modules:
  0.0 554.2 jit_solution(11933551284616293787)
XLA Ops:
  6.5 0.0 reduce-scatter.2.cloned.1.call-start
  6.5 1.6 slice.156
  8.2 1.3 collective-permute-start
  9.5 0.7 iota_add_fusion
  10.2 1.7 fusion.83
  11.9 1.3 compare_select_fusion.1
  13.2 0.8 fusion.43
  14.0 0.0 collective-permute-done
  14.1 0.0 copy-done.13
  14.1 6.2 %concatenate.3 = bf16[2,32,3,9792]{3,1,2,0:T(8,128)(2,1)} concatenate(bf16[2,32,3,4608]{3,1,2,0:T(8,128)(2,1)S(1)} %copy-done.13, bf16[2,32,3,3904]{3,1,2,0:T(8,128)(2,1)} %collective-permute-done, bf16[2,32,3,1280]{3,1,2,0:T(8,128)(2,1)S(1)} %broadcast_in_dim.2), dimensions={3} | concatenate | bytes 7520256 | tf_op jit(solution)/shard_map/concatenate | solution.py:25
  20.3 9.5 %fusion.82 = (bf16[2,32,3,9216]{3,1,2,0:T(8,128)(2,1)}, bf16[2,32,3,9216]{3,1,2,0:T(8,128)(2,1)S(1)}, bf16[2,32,3,9216]{3,1,2,0:T(8,128)(2,1)}, bf16[2,32,3,9216]{3,1,2,0:T(8,128)(2,1)}) fusion(bf16[2,32,3,9792]{3,1,2,0:T(8,128)(2,1)} %concatenate.3), kind=kLoop, calls=%fused_computation.133 | loop fusion | bytes 28311552 | tf_op jit(solution)/shard_map/slice | solution.py:31
  29.8 10.5 %stack_reshape.12 = bf16[2,32,3,12,3,1,256]{6,4,3,1,2,0,5:T(4,128)(2,1)} reshape(bf16[2,32,3,9216]{3,1,2,0:T(8,128)(2,1)} %get-tuple-element.26) | data formatting | bytes 7077888 | tf_op jit(solution)/shard_map/stack;reshape | solution.py:33
  40.3 6.2 %copy_dynamic-update-slice_fusion.3 = bf16[2,32,3,12,3,4,256]{6,1,5,4,3,2,0:T(8,128)(2,1)} fusion(bf16[2,32,3,12,3,1,256]{6,4,3,1,2,0,5:T(4,128)(2,1)} %stack_reshape.12), kind=kLoop, calls=%fused_computation.53 | loop fusion | bytes 7077888
  46.5 10.5 %stack_reshape.13 = bf16[2,32,3,12,3,1,256]{6,4,3,1,2,0,5:T(4,128)(2,1)} reshape(bf16[2,32,3,9216]{3,1,2,0:T(8,128)(2,1)} %get-tuple-element.25) | data formatting | bytes 7077888 | tf_op jit(solution)/shard_map/stack;reshape | solution.py:33
  57.1 7.6 %stack_reshape.14 = bf16[2,32,3,12,3,1,256]{6,4,3,1,2,0,5:T(4,128)(2,1)} reshape(bf16[2,32,3,9216]{3,1,2,0:T(8,128)(2,1)S(1)} %get-tuple-element.24) | data formatting | bytes 7077888 | tf_op jit(solution)/shard_map/stack;reshape | solution.py:33
  64.6 10.6 %stack_reshape.15 = bf16[2,32,3,12,3,1,256]{6,4,3,1,2,0,5:T(4,128)(2,1)} reshape(bf16[2,32,3,9216]{3,1,2,0:T(8,128)(2,1)} %get-tuple-element.23) | data formatting | bytes 7077888 | tf_op jit(solution)/shard_map/stack;reshape | solution.py:33
  75.2 6.4 %copy_dynamic-update-slice_fusion.2 = bf16[2,32,3,12,3,4,256]{6,1,5,4,3,2,0:T(8,128)(2,1)} fusion(bf16[2,32,3,12,3,4,256]{6,1,5,4,3,2,0:T(8,128)(2,1)} %copy_dynamic-update-slice_fusion.3, bf16[2,32,3,12,3,1,256]{6,4,3,1,2,0,5:T(4,128)(2,1)} %stack_reshape.13), kind=kLoop, calls=%fused_computation.52 | loop fusion | bytes 8257536
  81.5 0.0 slice-done
  81.6 3.8 copy_dynamic-update-slice_fusion.1
  85.4 0.0 slice-done.3
  85.4 3.8 copy_dynamic-update-slice_fusion
  89.2 27.2 %fusion.81 = (bf16[2,32,3,6,1,4,256]{6,1,5,4,3,2,0:T(8,128)(2,1)}, bf16[2,32,3,6,1,4,256]{6,1,5,4,3,2,0:T(8,128)(2,1)S(1)}, bf16[2,32,3,6,1,4,256]{6,1,5,4,3,2,0...) fusion(bf16[2,32,3,12,3,4,256]{6,1,5,4,3,2,0:T(8,128)(2,1)} %co, ...), kind=kLoop, calls=%fused_computation.132 | loop fusion | bytes 75497472 | tf_op jit(solution)/shard_map/slice | solution.py:39
  116.5 4.5 convert.35
  121.0 0.0 copy-done.12
  121.0 2.8 convert.36
  123.8 2.8 convert.37
  126.6 2.7 convert.38
  129.3 2.7 convert.39
  132.0 2.7 convert.40
  134.7 2.7 convert.41
  137.4 2.8 convert.42
  140.2 2.7 convert.43
  142.9 2.8 convert.44
  145.7 2.7 convert.45
  148.4 2.7 convert.46
  151.1 2.7 convert.47
  153.8 2.7 convert.48
  156.5 2.7 convert.49
  159.3 2.7 convert.50
  162.1 76.8 %fusion.10 = bf16[2,32,3,24,256]{4,3,2,1,0:T(8,128)(2,1)S(1)} fusion(f32[2,32,3,24,256]{4,1,3,2,0:T(8,128)} %convert.50, f32[2,32,3,24,256]{4,1,3,2,0:T(8,128)} %convert.49, f32[2,32,3,24,256]{4,1,3,2,0:T(8,128)} %convert.48, f32[2,32,3,24,256]{4,1,3,2,0:T(8,128)} %convert.47, f32[2,32,3,24,256]{4,1,3,2,0:T(8,128)} %convert.46, ...), kind=kLoop, calls=%fused_computation.20 | loop fusion | flops 37748736 | bytes 77873152 | tf_op jit(solution)/shard_map/convert_element_type | solution.py:44
  238.9 1.4 fusion.26
  240.4 0.0 copy-start.15
  240.4 1.4 fusion.25
  241.8 1.5 convolution_subtract_fusion
  243.3 0.0 copy-done.15
  243.3 0.0 copy-done.16
  243.3 1.9 subtract_convert_fusion.1
  245.3 0.0 copy-start.35
  245.3 4.5 copy.104
  249.8 4.4 copy.103
  254.2 0.0 copy-done.35
  254.2 51.2 %fusion.4 = f32[3,256,24,32]{3,2,1,0:T(8,128)S(1)} fusion(bf16[32,3,24,256]{0,2,3,1:T(8,128)(2,1)} %copy.104, f32[32,32]{1,0:T(8,128)S(1)} %get-tuple-element.46, s32[3,256]{1,0:T(4,128)S(1)} %copy-done.18, s32[32,32]{1,0:T(8,128)S(1)} %copy-done.35), kind=kOutput, calls=%fused_computation.13 | convolution fusion | flops 50331648 | bytes 3550208 | tf_op jit(solution)/shard_map/bsck,scfk->bcfk/dot_general | solution.py:97
  305.4 52.7 %fusion.3 = f32[3,256,24,32]{3,2,1,0:T(8,128)} fusion(bf16[32,3,24,256]{0,2,3,1:T(8,128)(2,1)S(1)} %copy-done.14, f32[32,32]{1,0:T(8,128)S(1)} %get-tuple-element.46, s32[3,256]{1,0:T(4,128)S(1)} %copy-done.18, s32[32,32]{1,0:T(8,128)S(1)} %copy-done.35), kind=kOutput, calls=%fused_computation.12 | convolution fusion | flops 50331648 | bytes 3550208 | tf_op jit(solution)/shard_map/bsck,scfk->bcfk/dot_general | solution.py:100
  358.1 54.0 %fusion.7 = bf16[32,1,3,24,256]{0,3,4,2,1:T(8,128)(2,1)} fusion(f32[3,256,24,32]{3,2,1,0:T(8,128)S(1)} %fusion.4, bf16[32,3,24,256]{0,2,3,1:T(8,128)(2,1)S(1)} %copy-done.14, s32[3,256]{1,0:T(4,128)S(1)} %copy-done.18, s32[32,32]{1,0:T(8,128)S(1)} %copy-done.35, f32[32,32]{1,0:T(8,128)S(1)} %copy-done.17), kind=kOutput, calls=%fused_computation.16 | convolution fusion | flops 51511296 | bytes 4729856 | tf_op jit(solution)/shard_map/bsck,scfk->bcfk/dot_general | solution.py:95
  412.2 5.6 %copy.107 = bf16[32,1,3,24,256]{4,3,2,1,0:T(8,128)(2,1)S(1)} copy(bf16[32,1,3,24,256]{0,3,4,2,1:T(8,128)(2,1)} %fusion.7) | data formatting | bytes 2359296 | tf_op jit(solution)/shard_map/stack | solution.py:101
  417.8 54.0 %fusion.8 = bf16[32,1,3,24,256]{0,3,4,2,1:T(8,128)(2,1)} fusion(f32[3,256,24,32]{3,2,1,0:T(8,128)} %fusion.3, bf16[32,3,24,256]{0,2,3,1:T(8,128)(2,1)} %copy.104, s32[3,256]{1,0:T(4,128)S(1)} %copy-done.18, s32[32,32]{1,0:T(8,128)S(1)} %copy-done.35, f32[32,32]{1,0:T(8,128)S(1)} %copy-done.17), kind=kOutput, calls=%fused_computation.17 | convolution fusion | flops 51511296 | bytes 4729856 | tf_op jit(solution)/shard_map/bsck,scfk->bcfk/dot_general | solution.py:98
  471.8 5.7 %copy.108 = bf16[32,1,3,24,256]{4,3,2,1,0:T(8,128)(2,1)S(1)} copy(bf16[32,1,3,24,256]{0,3,4,2,1:T(8,128)(2,1)} %fusion.8) | data formatting | bytes 2359296 | tf_op jit(solution)/shard_map/stack | solution.py:101
  477.5 1.6 pad_maximum_fusion
  479.1 0.0 reduce-scatter.2.cloned.1.call-update
  479.1 42.2 %reduce-scatter.2.cloned.1.call-done = bf16[8,2,3,24,256]{4,3,2,1,0:T(8,128)(2,1)} async-done(((bf16[32,2,3,24,256]{4,3,2,1,0:T(8,128)(2,1)}), bf16[8,2,3,24,256]{4,3,2,1,0:T(8,128)(2,1)}) %reduce-scatter.2.cloned.1.call-update) | async-done | bytes 589840 | tf_op jit(solution)/shard_map/reduce_scatter | solution.py:123
  521.3 20.3 %all_to_all.27 = bf16[8,2,3,24,256]{4,3,2,1,0:T(8,128)(2,1)S(1)} all-to-all(bf16[8,2,3,24,256]{4,3,2,1,0:T(8,128)(2,1)} %reduce-scatter.2.cloned.1.call-done), channel_id=1, replica_groups=mesh['stn'=4,'chan'=4,'beam'=2] {'chan'}, dimensions={0} | all-to-all | bytes 1179648 | tf_op jit(solution)/shard_map/all_to_all | solution.py:130
  541.7 4.2 all_to_all.28
  545.9 0.1 convert_bitcast_fusion
  546.0 1.2 copy.110
  (78 shorter events, 0.2 us)
Async XLA Ops:
  6.5 7.5 %copy-start.13 = (bf16[2,32,3,4608]{3,1,2,0:T(8,128)(2,1)S(1)}, bf16[2,32,3,4608]{3,1,2,0:T(8,128)(2,1)}, u32[]{:S(2)}) copy-start(bf16[2,32,3,4608]{3,1,2,0:T(8,128)(2,1)} %param.5) | copy-start | bytes 5308420
  6.5 514.8 %reduce-scatter.2.cloned.1.call-start = ((), (), s32[]{:S(2)}) async-start(), calls=%async_computation.3 | async-start | bytes 2949120 | tf_op jit(solution)/shard_map/reduce_scatter | solution.py:123
  8.2 5.8 %collective-permute-start = (bf16[2,32,3,3904]{3,1,2,0:T(8,128)(2,1)S(1)}, bf16[2,32,3,3904]{3,1,2,0:T(8,128)(2,1)}, u32[]{:S(2)}, u32[]{:S(2)}) collective-permute-start(bf16[2,32,3,3904]{3,1,2,0:T(8,128)(2,1)S(1)} %slice.156), channel_id=1, source_target_pairs={{1,0},{3,2},{5,4},{7,6},{9,8},{11,10},{13,12},{15,14},{17,16},{19,... | collective-permute-start | bytes 4497416 | tf_op jit(solution)/shard_map/ppermute | solution.py:14
  64.6 16.9 %slice-start = ((s8[4718592]{0:T(1024)(128)(4,1)}), s8[524288]{0:T(1024)(128)(4,1)S(1)}, s32[]{:S(2)}) async-start(s8[4718592]{0:T(1024)(128)(4,1)} %bitcast.115), calls=%async_computation.4 | async-start | bytes 1048576
  75.2 6.4 %slice-start.1 = ((s8[4718592]{0:T(1024)(128)(4,1)}), s8[4194304]{0:T(1024)(128)(4,1)S(1)}, s32[]{:S(2)}) async-start(s8[4718592]{0:T(1024)(128)(4,1)} %bitcast.115), calls=%async_computation.5 | async-start | bytes 8388608
  75.2 10.2 %slice-start.2 = ((s8[4718592]{0:T(1024)(128)(4,1)}), s8[4194304]{0:T(1024)(128)(4,1)S(1)}, s32[]{:S(2)}) async-start(s8[4718592]{0:T(1024)(128)(4,1)} %bitcast.117), calls=%async_computation.6 | async-start | bytes 8388608
  81.6 3.8 slice-start.3
  116.5 4.5 copy-start.12
  121.0 2.8 copy-start.11
  123.8 2.8 copy-start.10
  126.6 2.7 copy-start.9
  129.3 2.7 copy-start.8
  132.0 2.7 copy-start.7
  134.7 2.7 copy-start.6
  137.4 2.8 copy-start.5
  140.2 2.7 copy-start.4
  142.9 2.8 copy-start.3
  145.7 2.7 copy-start.2
  148.4 2.7 copy-start.1
  151.1 2.7 copy-start
  159.2 2.8 copy-start.19
  159.2 2.8 copy-start.20
  159.2 2.8 copy-start.21
  159.2 2.8 copy-start.22
  159.2 2.8 copy-start.23
  159.2 2.8 copy-start.24
  159.2 2.8 copy-start.25
  159.2 2.8 copy-start.26
  159.2 2.8 copy-start.27
  159.3 2.8 copy-start.28
  159.3 2.8 copy-start.29
  159.3 2.8 copy-start.30
  159.3 2.8 copy-start.31
  159.3 2.8 copy-start.32
  159.3 2.8 copy-start.33
  159.3 2.8 copy-start.34
  240.4 3.0 copy-start.15
  240.4 2.9 copy-start.16
  245.3 8.9 %copy-start.18 = (s32[3,256]{1,0:T(4,128)S(1)}, s32[3,256]{1,0:T(4,128)}, u32[]{:S(2)}) copy-start(s32[3,256]{1,0:T(4,128)} %iota_add_fusion) | copy-start | bytes 9220
  245.3 8.9 %copy-start.35 = (s32[32,32]{1,0:T(8,128)S(1)}, s32[32,32]{1,0:T(8,128)}, u32[]{:S(2)}) copy-start(s32[32,32]{1,0:T(8,128)} %param.7) | copy-start | bytes 12292
  254.2 51.2 %copy-start.14 = (bf16[32,3,24,256]{0,2,3,1:T(8,128)(2,1)S(1)}, bf16[32,3,24,256]{0,2,3,1:T(8,128)(2,1)}, u32[]{:S(2)}) copy-start(bf16[32,3,24,256]{0,2,3,1:T(8,128)(2,1)} %copy.103) | copy-start | bytes 3538948
  305.4 52.8 %copy-start.17 = (f32[32,32]{1,0:T(8,128)S(1)}, f32[32,32]{1,0:T(8,128)}, u32[]{:S(2)}) copy-start(f32[32,32]{1,0:T(8,128)} %get-tuple-element.45) | copy-start | bytes 12292
Sparse Core Ops, SparseCore 0:
  479.3 41.9 reduce-scatter.1
where the time goes:
time: 564 us; the launch traced here: 554 us
  matrix products  218 us (39%)
  local copies, waits for them, and re-layouts  127 us (23%)
  other arithmetic  127 us (23%)
  waiting for transfers between devices  42.2 us (7%)
  blocking collectives  24.5 us (4%)
  between operations  14.1 us (2%)
    convert_element_type x1, other arithmetic, filter_frames(): return total.reshape(shape[:-1] + (frame_count, fine)).astype(jnp.bfloat16)  76.8 us
    dot_general x1, matrix products, complex_form(): jnp.einsum(form, weight_re, pieces[0], preferred_element_type=jnp.float32)  54 us
    dot_general x1, matrix products, complex_form(): jnp.einsum(form, weight_re, pieces[1], preferred_element_type=jnp.float32)  54 us
    dot_general x1, matrix products, complex_form(): jnp.einsum(form, weight_im, pieces[0], preferred_element_type=jnp.float32)  52.7 us
    dot_general x1, matrix products, complex_form(): jnp.einsum(form, weight_im, pieces[1], preferred_element_type=jnp.float32)  51.2 us
    convert_element_type x16, other arithmetic, filter_frames(): lax.slice_in_dim(stacked, lead, lead + groups, 1, axis)[..., inner, :, :]  45.3 us
    another operation x5, local copies, waits for them, and re-layouts, filter_frames(): stacked = jnp.stack(streams, axis=-2)  43 us
    reduce_scatter x1, waiting for transfers between devices, body(): lax.psum_scatter(complex_form(weight_re, weight_im, spectra).astype(jnp.b...  42.2 us
  transfers between devices with their start and end apart: 2, of which 1 were waited for; matrix products, arithmetic and copies ran while one was open for 1% of the time, Pallas kernels for 0%

commit v1 on v0

v1 whole, which is shorter than its diff:
```python
import functools
import math

import jax
import jax.numpy as jnp
import numpy as np
from jax import lax
from jax.experimental import pallas as pl
from jax.experimental.pallas import tpu as pltpu
from jax.sharding import PartitionSpec as P

SUBARRAYS = 4
UNROLL = 4
LANES = 128


def dft_tables(fine):
    index = np.arange(fine)
    angle = 2.0 * np.pi * (index[:, None] * index[None, :] % fine) / fine
    scale = 1.0 / math.sqrt(fine)
    return (
        jnp.asarray(np.cos(angle) * scale, jnp.bfloat16),
        jnp.asarray(np.sin(angle) * scale, jnp.bfloat16),
    )


def unit_turn(turn):
    quarter = (turn + 8192) >> 14
    t = (turn - (quarter << 14)).astype(jnp.float32) * (2.0 * math.pi / 65536.0)
    u = t * t
    sine = t * (1.0 + u * (-1.0 / 6 + u * (1.0 / 120 + u * (-1.0 / 5040))))
    cosine = 1.0 + u * (-0.5 + u * (1.0 / 24 + u * (-1.0 / 720 + u * (1.0 / 40320))))
    odd = (quarter & 1) == 1
    c = jnp.where(odd, sine, cosine)
    s = jnp.where(odd, cosine, sine)
    c = jnp.where(((quarter + 1) & 2) == 2, -c, c)
    s = jnp.where((quarter & 2) == 2, -s, s)
    return c, s


def beam_kernel(
    amplitude,
    station_sub,
    beam_sub,
    start,
    delay_ref,
    taps_ref,
    cos_ref,
    sin_ref,
    own_ref,
    next_ref,
    out_ref,
    table,
    wide,
    half,
    filtered,
    spec,
    x_ref,
    w_ref,
    members,
    counts,
):
    tap_count, fine = taps_ref.shape
    stations = own_ref.shape[2]
    samples = own_ref.shape[3]
    beams = out_ref.shape[0]
    frames = out_ref.shape[3]
    groups = frames // 4
    parts = fine // LANES
    row = stations + UNROLL
    chan = pl.program_id(0)

    @pl.when(chan == 0)
    def _():
        for sub in range(SUBARRAYS):
            def add(s, n, sub=sub):
                members[sub * row + n] = s
                return n + jnp.where(station_sub[s] == sub, 1, 0)

            count = lax.fori_loop(0, stations, add, jnp.int32(0))
            for extra in range(UNROLL):
                members[sub * row + count + extra] = stations
            counts[sub] = (count + UNROLL - 1) // UNROLL
        for part in range(2 * parts):
            x_ref[part, stations] = jnp.zeros((frames, LANES), jnp.float32)
            w_ref[part, pl.ds(stations, 8), :] = jnp.zeros((8, LANES), jnp.float32)
        cosine = cos_ref[...].astype(jnp.float32)
        sine = sin_ref[...].astype(jnp.float32)
        k = lax.broadcasted_iota(jnp.int32, (fine, fine), 1)
        for phase in range(4):
            q = (3 * phase * k) & 3
            cq = jnp.where(q == 0, 1.0, jnp.where(q == 2, -1.0, 0.0))
            sq = jnp.where(q == 1, 1.0, jnp.where(q == 3, -1.0, 0.0))
            same = (cosine * cq - sine * sq).astype(jnp.bfloat16)
            cross = sine * cq + cosine * sq
            table[phase, 0:fine, 0:fine] = same
            table[phase, fine:, fine:] = same
            table[phase, fine:, 0:fine] = cross.astype(jnp.bfloat16)
            table[phase, 0:fine, fine:] = (-cross).astype(jnp.bfloat16)

    for ri in range(2):
        wide[ri, :, 0:samples] = own_ref[ri, 0].astype(jnp.float32)
        wide[ri, :, samples:] = next_ref[ri, 0].astype(jnp.float32)
        shift = fine // 4
        length = half.shape[2]
        half[ri] = wide[ri, :, shift : shift + length]

    hop = 3 * fine // 4

    @pl.loop(0, groups)
    def _(g):
        for phase in range(4):
            source = wide if phase % 2 == 0 else half
            base = phase * hop - (0 if phase % 2 == 0 else fine // 4)
            for ri in range(2):
                total = None
                for tap in range(tap_count):
                    at = pl.multiple_of(g * 3 * fine + (base + tap * fine), LANES)
                    term = taps_ref[tap : tap + 1, :] * source[ri, :, pl.ds(at, fine)]
                    total = term if total is None else total + term
                filtered[phase, pl.ds(pl.multiple_of(g * stations, stations), stations), ri * fine : (ri + 1) * fine] = (
                    total.astype(jnp.bfloat16)
                )

    for phase in range(4):
        result = jnp.dot(filtered[phase], table[phase], preferred_element_type=jnp.float32)
        for g in range(groups):
            at = (4 * g + phase) * stations
            for part in range(2 * parts):
                spec[part, at : at + stations, :] = result[
                    g * stations : (g + 1) * stations, part * LANES : (part + 1) * LANES
                ]
    for s in range(stations):
        for part in range(2 * parts):
            x_ref[part, s] = spec.at[part][pl.ds(s, frames, stride=stations), :]

    lane = lax.broadcasted_iota(jnp.int32, (stations, LANES), 1)
    first = (start[0] + chan) * fine

    @pl.loop(0, beams)
    def _(b):
        delay = delay_ref[b]
        for part in range(parts):
            turn = (delay * (lane + (first + part * LANES))) & 65535
            c, s = unit_turn(turn)
            w_ref[part, 0:stations, :] = c * amplitude
            w_ref[parts + part, 0:stations, :] = s * (-amplitude)
        sub = beam_sub[b]

        def add(i, carry):
            totals = list(carry)
            for u in range(UNROLL):
                s = members[sub * row + i * UNROLL + u]
                for part in range(parts):
                    w_re = w_ref.at[part][pl.ds(s, 8, stride=0), :][None]
                    w_im = w_ref.at[parts + part][pl.ds(s, 8, stride=0), :][None]
                    x_re = x_ref[part, s].reshape(frames // 8, 8, LANES)
                    x_im = x_ref[parts + part, s].reshape(frames // 8, 8, LANES)
                    totals[part] = totals[part] + (w_re * x_re - w_im * x_im)
                    totals[parts + part] = totals[parts + part] + (w_re * x_im + w_im * x_re)
            return tuple(totals)

        zero = jnp.zeros((frames // 8, 8, LANES), jnp.float32)
        totals = lax.fori_loop(0, counts[sub], add, (zero,) * (2 * parts))
        for part in range(parts):
            lanes = slice(part * LANES, (part + 1) * LANES)
            out_ref[b, 0, 0, :, lanes] = totals[part].reshape(frames, LANES).astype(jnp.bfloat16)
            out_ref[b, 1, 0, :, lanes] = totals[parts + part].reshape(frames, LANES).astype(jnp.bfloat16)


def beam_sums(own, following, taps, delays, station_sub, beam_sub, chan_start, amplitude):
    tap_count, fine = taps.shape
    chans, stations, samples = own.shape[1:]
    beams = delays.shape[0]
    hop = 3 * fine // 4
    frames = samples // hop
    parts = fine // LANES
    cosine, sine = dft_tables(fine)
    delay = jnp.broadcast_to(delays[:, :, None], (beams, stations, LANES))
    whole = lambda *shape: pl.BlockSpec(shape, lambda c, *_: (0,) * len(shape))
    volts_spec = pl.BlockSpec((2, 1, stations, samples), lambda c, *_: (0, c, 0, 0))
    length = 2 * samples - LANES
    return pl.pallas_call(
        functools.partial(beam_kernel, amplitude),
        out_shape=jax.ShapeDtypeStruct((beams, 2, chans, frames, fine), jnp.bfloat16),
        grid_spec=pltpu.PrefetchScalarGridSpec(
            num_scalar_prefetch=3,
            grid=(chans,),
            in_specs=[
                whole(beams, stations, LANES),
                whole(tap_count, fine),
                whole(fine, fine),
                whole(fine, fine),
                volts_spec,
                volts_spec,
            ],
            out_specs=pl.BlockSpec((beams, 2, 1, frames, fine), lambda c, *_: (0, 0, c, 0, 0)),
            scratch_shapes=[
                pltpu.VMEM((4, 2 * fine, 2 * fine), jnp.bfloat16),
                pltpu.VMEM((2, stations, 2 * samples), jnp.float32),
                pltpu.VMEM((2, stations, length), jnp.float32),
                pltpu.VMEM((4, frames // 4 * stations, 2 * fine), jnp.bfloat16),
                pltpu.VMEM((2 * parts, (frames + 1) * stations, LANES), jnp.float32),
                pltpu.VMEM((2 * parts, stations + 1, frames, LANES), jnp.float32),
                pltpu.VMEM((2 * parts, stations + 8, LANES), jnp.float32),
                pltpu.SMEM((SUBARRAYS * (stations + UNROLL),), jnp.int32),
                pltpu.SMEM((SUBARRAYS,), jnp.int32),
            ],
        ),
        compiler_params=pltpu.CompilerParams(dimension_semantics=("arbitrary",)),
        name="beam_sums",
    )(station_sub, beam_sub, chan_start, delay, taps, cosine, sine, own, following)


def body(volts, taps, delays, station_sub, beam_sub):
    own = jnp.transpose(volts, (0, 2, 1, 3))
    size = lax.axis_size("beam")
    following = lax.ppermute(own, "beam", [(i, i - 1) for i in range(1, size)])
    chans = own.shape[1]
    chan_start = (lax.axis_index("chan") * chans).astype(jnp.int32)[None]
    stations = delays.shape[1] * lax.axis_size("stn")
    amplitude = 1.0 / math.sqrt(stations // SUBARRAYS)
    partial = beam_sums(
        own, following, taps, delays, station_sub, beam_sub, chan_start, amplitude
    )
    summed = lax.psum_scatter(partial, "stn", scatter_dimension=0, tiled=True)
    swapped = lax.all_to_all(summed, "chan", split_axis=0, concat_axis=2, tiled=True)
    swapped = lax.all_to_all(swapped, "beam", split_axis=0, concat_axis=3, tiled=True)
    return swapped.astype(jnp.float32)


def solution(mesh):
    placed = (P(None, "stn", "chan", "beam"), P(), P(None, "stn"), P("stn"), P())
    return jax.shard_map(
        body,
        mesh=mesh,
        in_specs=placed,
        out_specs=P(("stn", "chan", "beam"), None, None, None, None),
        check_vma=False,
    )
```

time: 564 us -> 116 us (0.21); the launches traced: 554 us -> 116 us
  matrix products: 218 us -> 0 us
  other arithmetic: 127 us -> 0.09 us
  local copies, waits for them, and re-layouts: 127 us -> 2.92 us
  Pallas kernels: 0 us -> 29.6 us
    dot_general x8 -> x0, matrix products: 218 us -> none  [the longest x1 54 us: complex_form(): jnp.einsum(form, weight_re, pieces[0], preferred_element_type=jnp.float32)]
    convert_element_type x18 -> x1, other arithmetic: 122 us -> 0.09 us  [body(): return swapped.astype(jnp.float32)]
    another operation x7 -> x0, local copies, waits for them, and re-layouts: 54.3 us -> none  [the longest x5 43 us: filter_frames(): stacked = jnp.stack(streams, axis=-2)]
    slice x4 -> x0, local copies, waits for them, and re-layouts: 40.1 us -> none  [the longest x1 27.2 us: filter_frames(): lax.slice_in_dim(stacked, lead, lead + groups, 1, axis)[..., inner, :, :]]
    pallas_call x0 -> x1, Pallas kernels: none -> 29.6 us  [beam_sums(): pl.pallas_call(functools.partial(beam_kernel, amplitude), out_shape=jax.S...]
    unnamed x83 -> x2, local copies, waits for them, and re-layouts: 16.6 us -> 0.01 us
    squeeze x2 -> x0, local copies, waits for them, and re-layouts: 8.92 us -> none  [the longest x1 4.48 us: complex_form(): pieces[1]]
    concatenate x1 -> x0, local copies, waits for them, and re-layouts: 6.21 us -> none  [filter_frames(): jnp.concatenate([extended, jnp.zeros(shape[:-1] + (padding,), extended.dt...]
  transfers between devices with their start and end apart: 2 -> 2, of which waited for: 1 -> 2; matrix products, arithmetic and copies ran while one was open for 1% -> 0% of each run, Pallas kernels for 0% -> 0%
where the time goes in v1:
time: 116 us
  waiting for transfers between devices  43.7 us (38%)
  Pallas kernels  29.6 us (26%)
  blocking collectives  24.5 us (21%)
  between operations  13.4 us (12%)
  local copies, waits for them, and re-layouts  2.92 us (3%)
  starting transfers between devices  1.28 us (1%)
    reduce_scatter x1, waiting for transfers between devices, body(): summed = lax.psum_scatter(partial, 'stn', scatter_dimension=0, tiled=True)  39.2 us
    pallas_call x1, Pallas kernels, beam_sums(): pl.pallas_call(functools.partial(beam_kernel, amplitude), out_shape=jax.S...  29.6 us
    all_to_all x1, blocking collectives, body(): lax.all_to_all(summed, 'chan', split_axis=0, concat_axis=2, tiled=True)  20.3 us
    ppermute x1, waiting for transfers between devices, body(): following = lax.ppermute(own, 'beam', [(i, i - 1) for i in range(1, size)])  4.49 us
    all_to_all x1, blocking collectives, body(): lax.all_to_all(swapped, 'beam', split_axis=0, concat_axis=3, tiled=True)  4.21 us
  transfers between devices with their start and end apart: 2, of which 2 were waited for; matrix products, arithmetic and copies ran while one was open for 0% of the time, Pallas kernels for 0%

profile of v1, /device:TPU:0, one launch (start us, length us, event | category | flops | bytes accessed | tf_op | source)
XLA Modules:
  0.0 115.5 jit_solution(16290720195843968192)
XLA Ops:
  6.5 0.0 reduce-scatter.2.cloned.1.call-start
  6.5 1.3 %collective-permute-start = (bf16[2,3,32,4608]{3,2,1,0:T(8,128)(2,1)}, bf16[2,3,32,4608]{3,2,1,0:T(8,128)(2,1)S(1)}, u32[]{:S(2)}, u32[]{:S(2)}) collective-permute-start(bf16[2,3,32,4608]{3,2,1,0:T(8,128)(2,1)} %bitcast.14), channel_id=1, source_target_pairs={{1,0},{3,2},{5,4},{7,6},{9,8},{11,10},{13,12},{15,14},{17,16},{19,... | collective-permute-start | bytes 5308424 | tf_op jit(solution)/shard_map/ppermute | solution.py:218
  7.8 4.5 %collective-permute-done.next_ref = bf16[2,3,32,4608]{3,2,1,0:T(8,128)(2,1)S(1)} collective-permute-done((bf16[2,3,32,4608]{3,2,1,0:T(8,128)(2,1)}, bf16[2,3,32,4608]{3,2,1,0:T(8,128)(2,1)S(1)}, u32[]{:S(2)}, u32[]{:S(2)}) %collective-permute-start) | collective-permute-done | bytes 1769504 | tf_op jit(solution)/shard_map/ppermute | solution.py:218
  12.3 0.0 copy-start
  12.3 1.7 %broadcast_in_dim.10.delay_ref = s32[32,32,128]{2,1,0:T(8,128)} broadcast(s32[32,32]{1,0:T(8,128)} %param.9), dimensions={0,1} | broadcast | bytes 528384 | tf_op jit(solution)/shard_map/broadcast_in_dim | solution.py:179
  14.0 0.0 copy-done
  14.0 29.6 %beam_sums.1 = bf16[32,2,3,24,256]{4,3,2,1,0:T(8,128)(2,1)} custom-call(s32[32]{0:T(128)} %station_sub.1, s32[32]{0:T(128)} %beam_sub.1, s32[1]{0:T(128)} %bitcast.start, s32[32,32,128]{2,1,0:T(8,128)} %broadcast_in_dim.10.delay_ref, f32[16,256]{1,0:T(8,128)} %taps_ref.1, bf16[256,256]{1,0:T(8,128)(2,1)} %constant.12.clone.cos_ref, ...), custom_call_target="tpu_custom_call" | custom-call | tf_op jit(solution)/shard_map/beam_sums/pallas_call | solution.py:183
  43.6 0.0 reduce-scatter.2.cloned.1.call-update
  43.6 39.2 %reduce-scatter.2.cloned.1.call-done = bf16[8,2,3,24,256]{4,3,2,1,0:T(8,128)(2,1)} async-done(((bf16[32,2,3,24,256]{4,3,2,1,0:T(8,128)(2,1)}), bf16[8,2,3,24,256]{4,3,2,1,0:T(8,128)(2,1)}) %reduce-scatter.2.cloned.1.call-update) | async-done | bytes 589840 | tf_op jit(solution)/shard_map/reduce_scatter | solution.py:226
  82.8 20.3 %all_to_all.27 = bf16[8,2,3,24,256]{4,3,2,1,0:T(8,128)(2,1)S(1)} all-to-all(bf16[8,2,3,24,256]{4,3,2,1,0:T(8,128)(2,1)} %reduce-scatter.2.cloned.1.call-done), channel_id=1, replica_groups=mesh['stn'=4,'chan'=4,'beam'=2] {'chan'}, dimensions={0} | all-to-all | bytes 1179648 | tf_op jit(solution)/shard_map/all_to_all | solution.py:227
  103.2 4.2 %all_to_all.28 = bf16[2,2,12,24,256]{4,3,2,1,0:T(8,128)(2,1)S(1)} all-to-all(bf16[2,2,12,24,256]{4,3,2,1,0:T(8,128)(2,1)S(1)} %bitcast.13), channel_id=1, replica_groups=mesh['stn'=4,'chan'=4,'beam'=2] {'beam'}, dimensions={0} | all-to-all | bytes 1179648 | tf_op jit(solution)/shard_map/all_to_all | solution.py:228
  107.4 0.1 convert_bitcast_fusion
  107.5 1.2 %copy.10 = f32[1,2,12,2,24,256]{5,4,3,2,1,0:T(8,128)} copy(f32[1,2,12,2,24,256]{5,4,2,1,3,0:T(8,128)S(1)} %convert_bitcast_fusion) | data formatting | bytes 2359296 | tf_op jit(solution)/shard_map/convert_element_type | solution.py:229
  (1 shorter events, 0.0 us)
Async XLA Ops:
  6.5 76.3 %reduce-scatter.2.cloned.1.call-start = ((), (), s32[]{:S(2)}) async-start(), calls=%async_computation.3 | async-start | bytes 2949120 | tf_op jit(solution)/shard_map/reduce_scatter | solution.py:226
  6.5 5.8 %collective-permute-start = (bf16[2,3,32,4608]{3,2,1,0:T(8,128)(2,1)}, bf16[2,3,32,4608]{3,2,1,0:T(8,128)(2,1)S(1)}, u32[]{:S(2)}, u32[]{:S(2)}) collective-permute-start(bf16[2,3,32,4608]{3,2,1,0:T(8,128)(2,1)} %bitcast.14), channel_id=1, source_target_pairs={{1,0},{3,2},{5,4},{7,6},{9,8},{11,10},{13,12},{15,14},{17,16},{19,... | collective-permute-start | bytes 5308424 | tf_op jit(solution)/shard_map/ppermute | solution.py:218
  12.3 1.7 %copy-start = (bf16[2,3,32,4608]{3,2,1,0:T(8,128)(2,1)}, bf16[2,3,32,4608]{3,2,1,0:T(8,128)(2,1)S(1)}, u32[]{:S(2)}) copy-start(bf16[2,3,32,4608]{3,2,1,0:T(8,128)(2,1)S(1)} %collective-permute-done.next_ref) | copy-start | bytes 5308420
Sparse Core Ops, SparseCore 0:
  43.7 39.0 reduce-scatter.1

commit v2 on v1

--- a/solution.py
+++ b/solution.py
@@ -12,6 +12,7 @@
 SUBARRAYS = 4
 UNROLL = 4
 LANES = 128
+MESH = pl.DeviceIdType.MESH
 
 
 def dft_tables(fine):
@@ -43,7 +44,7 @@
     station_sub,
     beam_sub,
     start,
-    delay_ref,
+    turns_ref,
     taps_ref,
     cos_ref,
     sin_ref,
@@ -57,14 +58,14 @@
     spec,
     x_ref,
     w_ref,
+    delay_ref,
     members,
     counts,
 ):
     tap_count, fine = taps_ref.shape
     stations = own_ref.shape[2]
     samples = own_ref.shape[3]
-    beams = out_ref.shape[0]
-    frames = out_ref.shape[3]
+    beams, frames = out_ref.shape[2:4]
     groups = frames // 4
     parts = fine // LANES
     row = stations + UNROLL
@@ -84,6 +85,8 @@
         for part in range(2 * parts):
             x_ref[part, stations] = jnp.zeros((frames, LANES), jnp.float32)
             w_ref[part, pl.ds(stations, 8), :] = jnp.zeros((8, LANES), jnp.float32)
+        for b in range(beams):
+            delay_ref[b] = jnp.broadcast_to(turns_ref[:, b : b + 1], (stations, LANES))
         cosine = cos_ref[...].astype(jnp.float32)
         sine = sin_ref[...].astype(jnp.float32)
         k = lax.broadcasted_iota(jnp.int32, (fine, fine), 1)
@@ -164,8 +167,8 @@
         totals = lax.fori_loop(0, counts[sub], add, (zero,) * (2 * parts))
         for part in range(parts):
             lanes = slice(part * LANES, (part + 1) * LANES)
-            out_ref[b, 0, 0, :, lanes] = totals[part].reshape(frames, LANES).astype(jnp.bfloat16)
-            out_ref[b, 1, 0, :, lanes] = totals[parts + part].reshape(frames, LANES).astype(jnp.bfloat16)
+            out_ref[0, 0, b, :, lanes] = totals[part].reshape(frames, LANES).astype(jnp.bfloat16)
+            out_ref[0, 1, b, :, lanes] = totals[parts + part].reshape(frames, LANES).astype(jnp.bfloat16)
 
 
 def beam_sums(own, following, taps, delays, station_sub, beam_sub, chan_start, amplitude):
@@ -176,25 +179,24 @@
     frames = samples // hop
     parts = fine // LANES
     cosine, sine = dft_tables(fine)
-    delay = jnp.broadcast_to(delays[:, :, None], (beams, stations, LANES))
     whole = lambda *shape: pl.BlockSpec(shape, lambda c, *_: (0,) * len(shape))
     volts_spec = pl.BlockSpec((2, 1, stations, samples), lambda c, *_: (0, c, 0, 0))
     length = 2 * samples - LANES
     return pl.pallas_call(
         functools.partial(beam_kernel, amplitude),
-        out_shape=jax.ShapeDtypeStruct((beams, 2, chans, frames, fine), jnp.bfloat16),
+        out_shape=jax.ShapeDtypeStruct((chans, 2, beams, frames, fine), jnp.bfloat16),
         grid_spec=pltpu.PrefetchScalarGridSpec(
             num_scalar_prefetch=3,
             grid=(chans,),
             in_specs=[
-                whole(beams, stations, LANES),
+                whole(stations, beams),
                 whole(tap_count, fine),
                 whole(fine, fine),
                 whole(fine, fine),
                 volts_spec,
                 volts_spec,
             ],
-            out_specs=pl.BlockSpec((beams, 2, 1, frames, fine), lambda c, *_: (0, 0, c, 0, 0)),
+            out_specs=pl.BlockSpec((1, 2, beams, frames, fine), lambda c, *_: (c, 0, 0, 0, 0)),
             scratch_shapes=[
                 pltpu.VMEM((4, 2 * fine, 2 * fine), jnp.bfloat16),
                 pltpu.VMEM((2, stations, 2 * samples), jnp.float32),
@@ -203,13 +205,157 @@
                 pltpu.VMEM((2 * parts, (frames + 1) * stations, LANES), jnp.float32),
                 pltpu.VMEM((2 * parts, stations + 1, frames, LANES), jnp.float32),
                 pltpu.VMEM((2 * parts, stations + 8, LANES), jnp.float32),
+                pltpu.VMEM((beams, stations, LANES), jnp.int32),
                 pltpu.SMEM((SUBARRAYS * (stations + UNROLL),), jnp.int32),
                 pltpu.SMEM((SUBARRAYS,), jnp.int32),
             ],
         ),
         compiler_params=pltpu.CompilerParams(dimension_semantics=("arbitrary",)),
         name="beam_sums",
-    )(station_sub, beam_sub, chan_start, delay, taps, cosine, sine, own, following)
+    )(station_sub, beam_sub, chan_start, delays.T, taps, cosine, sine, own, following)
+
+
+def exchange_kernel(sizes, part_ref, out_ref, *scratch):
+    n_chan, n_core, bits = sizes
+    received, sent = scratch[:bits], scratch[bits : 2 * bits - 1]
+    total, send, recv, far_send, far_recv, own_sem = scratch[2 * bits - 1 :]
+    chans = part_ref.shape[0]
+    per_device = total.shape[3]
+    stn, chan, core = (lax.axis_index(name) for name in ("stn", "chan", "beam"))
+    own_bit = [(stn // 2 ** (bits - 1 - dim)) % 2 for dim in range(bits)]
+    orders = (tuple(range(bits - 1, -1, -1)), tuple(range(bits)))
+
+    def partner(dim):
+        return (stn + (1 - 2 * own_bit[dim]) * 2 ** (bits - 1 - dim), chan, core)
+
+    def far(dz, dc):
+        return ((chan + dz) % n_chan, (core + dc) % n_core)
+
+    offsets = [(dz, dc) for dz in range(n_chan) for dc in range(n_core)]
+    barrier = pltpu.get_barrier_semaphore()
+    peers = [partner(dim) for dim in range(bits)] + [(stn, *far(dz, dc)) for dz, dc in offsets[1:]]
+    for peer in peers:
+        pl.semaphore_signal(barrier, inc=1, device_id=peer, device_id_type=MESH)
+    pl.semaphore_wait(barrier, len(peers))
+
+    def region(ri, stage, last):
+        order = orders[ri]
+        index = [slice(None)] * bits
+        for dim in order[:stage]:
+            index[dim] = own_bit[dim]
+        if stage < bits:
+            index[order[stage]] = last(order[stage])
+        return index
+
+    def other(dim):
+        return 1 - own_bit[dim]
+
+    def with_received(c, ri, stage, index):
+        value = part_ref[(c, ri, *index)].astype(jnp.float32)
+        for earlier in range(stage):
+            kept = [dim for dim in range(bits) if dim not in orders[ri][: earlier + 1]]
+            piece = received[earlier][(c, ri, *(index[dim] for dim in kept))]
+            value = value + piece.astype(jnp.float32)
+        return value
+
+    def hop(c, ri, stage):
+        if stage == 0:
+            source = part_ref.at[(c, ri, *region(ri, 0, other))]
+        else:
+            source = sent[stage - 1].at[c, ri]
+        return pltpu.make_async_remote_copy(
+            src_ref=source,
+            dst_ref=received[stage].at[c, ri],
+            send_sem=send.at[stage, c, ri],
+            recv_sem=recv.at[stage, c, ri],
+            device_id=partner(orders[ri][stage]),
+            device_id_type=MESH,
+        )
+
+    def deliver(c, number):
+        z, k = far(*offsets[number])
+        return pltpu.make_async_remote_copy(
+            src_ref=total.at[c, z, k],
+            dst_ref=out_ref.at[:, :, chan * chans + c, core],
+            send_sem=far_send.at[c, number],
+            recv_sem=far_recv.at[c, number],
+            device_id=(stn, z, k),
+            device_id_type=MESH,
+        )
+
+    def keep(c):
+        return pltpu.make_async_copy(
+            total.at[c, chan, core], out_ref.at[:, :, chan * chans + c, core], own_sem.at[c]
+        )
+
+    def step(c, stage):
+        if stage == 0:
+            for ri in range(2):
+                hop(c, ri, 0).start()
+            return
+        for ri in range(2):
+            hop(c, ri, stage - 1).wait_recv()
+            if stage < bits:
+                sent[stage - 1][c, ri] = with_received(
+                    c, ri, stage, region(ri, stage, other)
+                ).astype(jnp.bfloat16)
+            else:
+                value = with_received(c, ri, stage, own_bit).astype(jnp.bfloat16)
+                value = value.reshape((n_chan, n_core, per_device) + value.shape[1:])
+                total[c, :, :, :, ri] = value
+        if stage < bits:
+            for ri in range(2):
+                hop(c, ri, stage).start()
+        else:
+            for number in range(len(offsets) - 1, 0, -1):
+                deliver(c, number).start()
+            keep(c).start()
+
+    for tick in range(chans + bits):
+        for c in reversed(range(chans)):
+            if 0 <= tick - c <= bits:
+                step(c, tick - c)
+
+    for c in range(chans):
+        for ri in range(2):
+            for stage in range(bits):
+                hop(c, ri, stage).wait_send()
+        for number in range(1, len(offsets)):
+            deliver(c, number).wait()
+        keep(c).wait()
+
+
+def exchange(partial):
+    chans, _, beams, frames, fine = partial.shape
+    n_stn, n_chan, n_core = (lax.axis_size(name) for name in ("stn", "chan", "beam"))
+    bits = n_stn.bit_length() - 1
+    assert n_stn == 2**bits
+    per = beams // n_stn
+    per_device = per // (n_chan * n_core)
+    peers = n_chan * n_core
+    block = (per, frames, fine)
+    halves = [pltpu.VMEM((chans, 2) + (2,) * (bits - 1 - t) + block, jnp.bfloat16) for t in range(bits)]
+    out = pl.pallas_call(
+        functools.partial(exchange_kernel, (n_chan, n_core, bits)),
+        out_shape=jax.ShapeDtypeStruct(
+            (per_device, 2, n_chan * chans, n_core, frames, fine), jnp.bfloat16
+        ),
+        in_specs=[pl.BlockSpec(memory_space=pltpu.VMEM)],
+        out_specs=pl.BlockSpec(memory_space=pl.ANY),
+        scratch_shapes=[
+            *halves,
+            *halves[1:],
+            pltpu.VMEM((chans, n_chan, n_core, per_device, 2, frames, fine), jnp.bfloat16),
+            pltpu.SemaphoreType.DMA((bits, chans, 2)),
+            pltpu.SemaphoreType.DMA((bits, chans, 2)),
+            pltpu.SemaphoreType.DMA((chans, peers)),
+            pltpu.SemaphoreType.DMA((chans, peers)),
+            pltpu.SemaphoreType.DMA((chans,)),
+        ],
+        compiler_params=pltpu.CompilerParams(collective_id=0, has_side_effects=True),
+        name="exchange",
+    )(partial.reshape((chans, 2) + (2,) * bits + block))
+    return out.reshape(per_device, 2, n_chan * chans, n_core * frames, fine)
 
 
 def body(volts, taps, delays, station_sub, beam_sub):
@@ -223,10 +369,7 @@
     partial = beam_sums(
         own, following, taps, delays, station_sub, beam_sub, chan_start, amplitude
     )
-    summed = lax.psum_scatter(partial, "stn", scatter_dimension=0, tiled=True)
-    swapped = lax.all_to_all(summed, "chan", split_axis=0, concat_axis=2, tiled=True)
-    swapped = lax.all_to_all(swapped, "beam", split_axis=0, concat_axis=3, tiled=True)
-    return swapped.astype(jnp.float32)
+    return exchange(partial).astype(jnp.float32)
 
 
 def solution(mesh):

time: 116 us -> 75.6 us (0.65)
  waiting for transfers between devices: 43.7 us -> 3.1 us
  Pallas kernels: 29.6 us -> 66 us
  blocking collectives: 24.5 us -> 0 us
  between operations: 13.4 us -> 0.02 us
  other arithmetic: 0.09 us -> 2.21 us
    reduce_scatter x1 -> x0, waiting for transfers between devices: 39.2 us -> none  [body(): summed = lax.psum_scatter(partial, 'stn', scatter_dimension=0, tiled=True)]
    pallas_call x0 -> x1, Pallas kernels: none -> 37.2 us  [exchange(): pl.pallas_call(functools.partial(exchange_kernel, (n_chan, n_core, bits))...]
    all_to_all x2 -> x0, blocking collectives: 24.5 us -> none  [the longest x1 20.3 us: body(): lax.all_to_all(summed, 'chan', split_axis=0, concat_axis=2, tiled=True)]
    unnamed x2 -> x3, local copies, waits for them, and re-layouts: 0.01 us -> 2.59 us
    convert_element_type x1, other arithmetic: 0.09 us -> 2.21 us  [body(): return exchange(partial).astype(jnp.float32)]
    broadcast_in_dim x1 -> x0, local copies, waits for them, and re-layouts: 1.71 us -> none  [beam_sums(): delay = jnp.broadcast_to(delays[:, :, None], (beams, stations, LANES))]
    ppermute x1, waiting for transfers between devices: 4.49 us -> 3.1 us  [body(): following = lax.ppermute(own, 'beam', [(i, i - 1) for i in range(1, size)])]
    convert_element_type x1 -> x0, local copies, waits for them, and re-layouts: 1.17 us -> none  [body(): return swapped.astype(jnp.float32)]
  transfers between devices with their start and end apart: 2 -> 1, of which waited for: 2 -> 1; matrix products, arithmetic and copies ran while one was open for 0% -> 2% of each run, Pallas kernels for 0% -> 0%
where the time goes in v2:
time: 75.6 us; the launch traced here: 75.2 us
  Pallas kernels  66 us (87%)
  waiting for transfers between devices  3.1 us (4%)
  local copies, waits for them, and re-layouts  2.59 us (3%)
  other arithmetic  2.21 us (3%)
  starting transfers between devices  1.28 us (2%)
    pallas_call x1, Pallas kernels, exchange(): pl.pallas_call(functools.partial(exchange_kernel, (n_chan, n_core, bits))...  37.2 us
    pallas_call x1, Pallas kernels, beam_sums(): pl.pallas_call(functools.partial(beam_kernel, amplitude), out_shape=jax.S...  28.8 us
    ppermute x1, waiting for transfers between devices, body(): following = lax.ppermute(own, 'beam', [(i, i - 1) for i in range(1, size)])  3.1 us
    unnamed x3, local copies, waits for them, and re-layouts  2.59 us
    convert_element_type x1, other arithmetic, body(): return exchange(partial).astype(jnp.float32)  2.21 us
  transfers between devices with their start and end apart: 1, of which 1 were waited for; matrix products, arithmetic and copies ran while one was open for 2% of the time, Pallas kernels for 0%

profile of v2, /device:TPU:0, one launch (start us, length us, event | category | flops | bytes accessed | tf_op | source)
XLA Modules:
  0.0 75.2 jit_solution(11812841173360079341)
XLA Ops:
  0.0 1.3 %collective-permute-start = (bf16[2,3,32,4608]{3,2,1,0:T(8,128)(2,1)}, bf16[2,3,32,4608]{3,2,1,0:T(8,128)(2,1)S(1)}, u32[]{:S(2)}, u32[]{:S(2)}) collective-permute-start(bf16[2,3,32,4608]{3,2,1,0:T(8,128)(2,1)} %bitcast.8), channel_id=1, source_target_pairs={{1,0},{3,2},{5,4},{7,6},{9,8},{11,10},{13,12},{15,14},{17,16},{19,... | collective-permute-start | bytes 5308424 | tf_op jit(solution)/shard_map/ppermute | solution.py:364
  1.3 1.4 %copy.8 = s32[32,32]{0,1:T(8,128)} copy(s32[32,32]{1,0:T(8,128)} %param.9) | data formatting | bytes 8192 | tf_op args[2]
  2.7 3.1 %collective-permute-done.next_ref = bf16[2,3,32,4608]{3,2,1,0:T(8,128)(2,1)S(1)} collective-permute-done((bf16[2,3,32,4608]{3,2,1,0:T(8,128)(2,1)}, bf16[2,3,32,4608]{3,2,1,0:T(8,128)(2,1)S(1)}, u32[]{:S(2)}, u32[]{:S(2)}) %collective-permute-start) | collective-permute-done | bytes 1769504 | tf_op jit(solution)/shard_map/ppermute | solution.py:364
  5.8 0.0 copy-start
  5.8 1.2 %copy-done = bf16[2,3,32,4608]{3,2,1,0:T(8,128)(2,1)} copy-done((bf16[2,3,32,4608]{3,2,1,0:T(8,128)(2,1)}, bf16[2,3,32,4608]{3,2,1,0:T(8,128)(2,1)S(1)}, u32[]{:S(2)}) %copy-start) | copy-done | bytes 1769496
  7.0 28.8 %beam_sums.1 = bf16[3,2,32,24,256]{4,3,2,1,0:T(8,128)(2,1)} custom-call(s32[32]{0:T(128)} %station_sub.1, s32[32]{0:T(128)} %beam_sub.1, s32[1]{0:T(128)} %bitcast.start, s32[32,32]{1,0:T(8,128)} %bitcast.10, f32[16,256]{1,0:T(8,128)} %taps_ref.1, bf16[256,256]{1,0:T(8,128)(2,1)} %constant.12.clone.cos_ref, bf16[256,256]{1,0:T(8,128)(2,1)} %constant.13.clone.sin_ref, ...), custom_call_target="tpu_custom_call" | custom-call | tf_op jit(solution)/shard_map/beam_sums/pallas_call | solution.py:185
  35.8 37.2 %exchange.1 = bf16[1,2,12,2,24,256]{5,4,3,2,1,0:T(8,128)(2,1)} custom-call(bf16[3,2,2,2,8,24,256]{6,5,4,3,2,1,0:T(8,128)(2,1)} %bitcast.7), custom_call_target="tpu_custom_call" | custom-call | tf_op jit(solution)/shard_map/exchange/pallas_call | solution.py:338
  73.0 2.2 %bitcast_convert_fusion = f32[1,2,12,48,256]{4,3,2,1,0:T(8,128)} fusion(bf16[1,2,12,2,24,256]{5,4,3,2,1,0:T(8,128)(2,1)} %exchange.1), kind=kLoop, calls=%fused_computation | loop fusion | flops 294912 | bytes 1769472 | tf_op jit(solution)/shard_map/convert_element_type | solution.py:372
Async XLA Ops:
  0.0 5.8 %collective-permute-start = (bf16[2,3,32,4608]{3,2,1,0:T(8,128)(2,1)}, bf16[2,3,32,4608]{3,2,1,0:T(8,128)(2,1)S(1)}, u32[]{:S(2)}, u32[]{:S(2)}) collective-permute-start(bf16[2,3,32,4608]{3,2,1,0:T(8,128)(2,1)} %bitcast.8), channel_id=1, source_target_pairs={{1,0},{3,2},{5,4},{7,6},{9,8},{11,10},{13,12},{15,14},{17,16},{19,... | collective-permute-start | bytes 5308424 | tf_op jit(solution)/shard_map/ppermute | solution.py:364
  5.8 1.2 %copy-start = (bf16[2,3,32,4608]{3,2,1,0:T(8,128)(2,1)}, bf16[2,3,32,4608]{3,2,1,0:T(8,128)(2,1)S(1)}, u32[]{:S(2)}) copy-start(bf16[2,3,32,4608]{3,2,1,0:T(8,128)(2,1)S(1)} %collective-permute-done.next_ref) | copy-start | bytes 5308420

commit v3 on v2

--- a/solution.py
+++ b/solution.py
@@ -12,6 +12,7 @@
 SUBARRAYS = 4
 UNROLL = 4
 LANES = 128
+VMEM_LIMIT = 32 * 2**20
 MESH = pl.DeviceIdType.MESH
 
 
@@ -210,7 +211,9 @@
                 pltpu.SMEM((SUBARRAYS,), jnp.int32),
             ],
         ),
-        compiler_params=pltpu.CompilerParams(dimension_semantics=("arbitrary",)),
+        compiler_params=pltpu.CompilerParams(
+            dimension_semantics=("arbitrary",), vmem_limit_bytes=VMEM_LIMIT
+        ),
         name="beam_sums",
     )(station_sub, beam_sub, chan_start, delays.T, taps, cosine, sine, own, following)
 
@@ -352,7 +355,9 @@
             pltpu.SemaphoreType.DMA((chans, peers)),
             pltpu.SemaphoreType.DMA((chans,)),
         ],
-        compiler_params=pltpu.CompilerParams(collective_id=0, has_side_effects=True),
+        compiler_params=pltpu.CompilerParams(
+            collective_id=0, has_side_effects=True, vmem_limit_bytes=VMEM_LIMIT
+        ),
         name="exchange",
     )(partial.reshape((chans, 2) + (2,) * bits + block))
     return out.reshape(per_device, 2, n_chan * chans, n_core * frames, fine)

time: 75.6 us -> 75.6 us (level)
  local copies, waits for them, and re-layouts: 2.59 us -> 6.1 us
  Pallas kernels: 66 us -> 63 us
  other arithmetic: 2.21 us -> 1.18 us
    unnamed x3 -> x13, local copies, waits for them, and re-layouts: 2.59 us -> 6.1 us
    pallas_call x1, Pallas kernels: 37.2 us -> 34.4 us  [exchange(): pl.pallas_call(functools.partial(exchange_kernel, (n_chan, n_core, bits))...]
    convert_element_type x1, other arithmetic: 2.21 us -> 1.18 us  [body(): return exchange(partial).astype(jnp.float32)]
  transfers between devices with their start and end apart: 1 -> 1, of which waited for: 1 -> 1; matrix products, arithmetic and copies ran while one was open for 2% -> 1% of each run, Pallas kernels for 0% -> 0%
where the time goes in v3:
time: 75.6 us; the launch traced here: 75.3 us
  Pallas kernels  63 us (83%)
  local copies, waits for them, and re-layouts  6.1 us (8%)
  waiting for transfers between devices  3.7 us (5%)
  starting transfers between devices  1.28 us (2%)
  other arithmetic  1.18 us (2%)
    pallas_call x1, Pallas kernels, exchange(): pl.pallas_call(functools.partial(exchange_kernel, (n_chan, n_core, bits))...  34.4 us
    pallas_call x1, Pallas kernels, beam_sums(): pl.pallas_call(functools.partial(beam_kernel, amplitude), out_shape=jax.S...  28.5 us
    unnamed x13, local copies, waits for them, and re-layouts  6.1 us
    ppermute x1, waiting for transfers between devices, body(): following = lax.ppermute(own, 'beam', [(i, i - 1) for i in range(1, size)])  3.7 us
  transfers between devices with their start and end apart: 1, of which 1 were waited for; matrix products, arithmetic and copies ran while one was open for 1% of the time, Pallas kernels for 0%

profile of v3, /device:TPU:0, one launch (start us, length us, event | category | flops | bytes accessed | tf_op | source)
XLA Modules:
  0.0 75.3 jit_solution(4086279190319873082)
XLA Ops:
  0.0 1.3 %collective-permute-start = (bf16[2,3,32,4608]{3,2,1,0:T(8,128)(2,1)}, bf16[2,3,32,4608]{3,2,1,0:T(8,128)(2,1)S(1)}, u32[]{:S(2)}, u32[]{:S(2)}) collective-permute-start(bf16[2,3,32,4608]{3,2,1,0:T(8,128)(2,1)} %bitcast.8), channel_id=1, source_target_pairs={{1,0},{3,2},{5,4},{7,6},{9,8},{11,10},{13,12},{15,14},{17,16},{19,... | collective-permute-start | bytes 5308424 | tf_op jit(solution)/shard_map/ppermute | solution.py:369
  1.3 0.8 %copy.8 = s32[32,32]{0,1:T(8,128)S(1)} copy(s32[32,32]{1,0:T(8,128)} %param.9) | data formatting | bytes 8192 | tf_op args[2]
  2.1 3.7 %collective-permute-done.next_ref = bf16[2,3,32,4608]{3,2,1,0:T(8,128)(2,1)S(1)} collective-permute-done((bf16[2,3,32,4608]{3,2,1,0:T(8,128)(2,1)}, bf16[2,3,32,4608]{3,2,1,0:T(8,128)(2,1)S(1)}, u32[]{:S(2)}, u32[]{:S(2)}) %collective-permute-start) | collective-permute-done | bytes 1769504 | tf_op jit(solution)/shard_map/ppermute | solution.py:369
  5.8 0.0 copy-start
  5.8 1.5 %copy-done = bf16[2,32,3,4608]{3,1,2,0:T(8,128)(2,1)S(1)} copy-done((bf16[2,32,3,4608]{3,1,2,0:T(8,128)(2,1)S(1)}, bf16[2,32,3,4608]{3,1,2,0:T(8,128)(2,1)}, u32[]{:S(2)}) %copy-start) | copy-done | bytes 1769496
  7.3 0.0 copy-start.1
  7.3 0.9 %copy-done.1 = bf16[256,256]{1,0:T(8,128)(2,1)S(1)} copy-done((bf16[256,256]{1,0:T(8,128)(2,1)S(1)}, bf16[256,256]{1,0:T(8,128)(2,1)}, u32[]{:S(2)}) %copy-start.1) | copy-done | bytes 131096
  8.2 0.0 copy-start.2
  8.2 0.9 %copy-done.2 = bf16[256,256]{1,0:T(8,128)(2,1)S(1)} copy-done((bf16[256,256]{1,0:T(8,128)(2,1)S(1)}, bf16[256,256]{1,0:T(8,128)(2,1)}, u32[]{:S(2)}) %copy-start.2) | copy-done | bytes 131096
  9.1 0.0 copy-start.3
  9.1 0.7 copy-done.3
  9.8 0.0 copy-start.4
  9.8 0.7 copy-done.4
  10.4 0.0 copy-start.5
  10.4 0.7 copy-done.5
  11.1 28.5 %beam_sums.1 = bf16[3,2,32,24,256]{4,3,2,1,0:T(8,128)(2,1)S(1)} custom-call(s32[32]{0:T(128)S(1)} %copy-done.4, s32[32]{0:T(128)S(1)} %copy-done.5, s32[1]{0:T(128)} %bitcast.start, s32[32,32]{1,0:T(8,128)S(1)} %bitcast.10, f32[16,256]{1,0:T(8,128)S(1)} %copy-done.3, bf16[256,256]{1,0:T(8,128)(2,1)S(1)} %copy-done.2, bf16[256,256]{1,0:T(8,128)(2,1)S(1)} %copy-done.1, ...), custom_call_target="tpu_custom_call" | custom-call | tf_op jit(solution)/shard_map/beam_sums/pallas_call | solution.py:186
  39.7 34.4 %exchange.1 = bf16[1,2,12,2,24,256]{5,4,3,2,1,0:T(8,128)(2,1)S(1)} custom-call(bf16[3,2,2,2,8,24,256]{6,5,4,3,2,1,0:T(8,128)(2,1)S(1)} %bitcast.7), custom_call_target="tpu_custom_call" | custom-call | tf_op jit(solution)/shard_map/exchange/pallas_call | solution.py:341
  74.1 1.2 %bitcast_convert_fusion = f32[1,2,12,48,256]{4,3,2,1,0:T(8,128)} fusion(bf16[1,2,12,2,24,256]{5,4,3,2,1,0:T(8,128)(2,1)S(1)} %exchange.1), kind=kLoop, calls=%fused_computation | loop fusion | flops 294912 | bytes 1769472 | tf_op jit(solution)/shard_map/convert_element_type | solution.py:377
Async XLA Ops:
  0.0 5.8 %collective-permute-start = (bf16[2,3,32,4608]{3,2,1,0:T(8,128)(2,1)}, bf16[2,3,32,4608]{3,2,1,0:T(8,128)(2,1)S(1)}, u32[]{:S(2)}, u32[]{:S(2)}) collective-permute-start(bf16[2,3,32,4608]{3,2,1,0:T(8,128)(2,1)} %bitcast.8), channel_id=1, source_target_pairs={{1,0},{3,2},{5,4},{7,6},{9,8},{11,10},{13,12},{15,14},{17,16},{19,... | collective-permute-start | bytes 5308424 | tf_op jit(solution)/shard_map/ppermute | solution.py:369
  5.8 1.5 %copy-start = (bf16[2,32,3,4608]{3,1,2,0:T(8,128)(2,1)S(1)}, bf16[2,32,3,4608]{3,1,2,0:T(8,128)(2,1)}, u32[]{:S(2)}) copy-start(bf16[2,32,3,4608]{3,1,2,0:T(8,128)(2,1)} %param.7) | copy-start | bytes 5308420
  7.3 0.9 %copy-start.1 = (bf16[256,256]{1,0:T(8,128)(2,1)S(1)}, bf16[256,256]{1,0:T(8,128)(2,1)}, u32[]{:S(2)}) copy-start(bf16[256,256]{1,0:T(8,128)(2,1)} %constant.13.clone.sin_ref) | copy-start | bytes 393220
  8.2 0.9 %copy-start.2 = (bf16[256,256]{1,0:T(8,128)(2,1)S(1)}, bf16[256,256]{1,0:T(8,128)(2,1)}, u32[]{:S(2)}) copy-start(bf16[256,256]{1,0:T(8,128)(2,1)} %constant.12.clone.cos_ref) | copy-start | bytes 393220
  9.1 0.7 copy-start.3
  9.8 0.7 copy-start.4
  10.4 0.7 copy-start.5
